TPU v7x, 32 devices: a whole 2x2x4 slice. The times are simulated.
32 devices in a mesh: row: 8 (over y, x, core), col: 4 (over z).
Axes of the slice: x: 2, y: 2, z: 4, core: 2. Of those that a mesh axis runs over, the one named last changes fastest.
Arguments:
- left_act: bfloat16 [32, 64, 256], P(None, 'col', 'row'), may hold values from -6 to 6
- right_act: bfloat16 [32, 64, 256], P(None, 'row', 'col'), may hold values from -6 to 6
- cotangent: bfloat16 [256, 256, 128], P('row', 'col'), may hold values from -4 to 4
- weight: bfloat16 [1024, 128], replicated, may hold values from -0.1875 to 0.1875
Outputs:
- grad_left: float32 [32, 64, 256], P(None, 'col', 'row')
- grad_right: float32 [32, 64, 256], P(None, 'row', 'col')
- grad_weight: float32 [1024, 128], P('row')
All inputs are finite; a program needn't handle non-finite values.
Results may differ from a plain program's by a relative error of at most 0.0029.
Values may be sent and summed in bfloat16 or wider, within the bound.
No kernel may reach another device: no remote copies, remote signals or barrier semaphores. Data moves between devices by JAX's collectives and lax.ppermute only.
A program may use at most 128 MiB of HBM per device.

v0:
```python
import functools

import jax
import jax.numpy as jnp
from jax import lax
from jax.experimental import pallas as pl
from jax.experimental.pallas import tpu as pltpu
from jax.sharding import PartitionSpec as P


F32 = jnp.float32
BF16 = jnp.bfloat16
STEPS = 4
VMEM = pl.BlockSpec(memory_space=pltpu.VMEM)
HBM = pl.BlockSpec(memory_space=pltpu.HBM)


def xor_permute(x, axis, size, k):
    return lax.ppermute(x, axis, [(r, r ^ k) for r in range(size)])


def near_slots(n_col):
    slots = [0]
    far = n_col // 2
    while far > 1:
        slots += [slot ^ far for slot in slots]
        far //= 2
    return slots


def prep_kernel(l_hbm, r_hbm, g_hbm, w_hbm, l_out, r_out, gbd_ref, wp, l_ref, r_ref, w_ref, sems):
    chans, _, ti = l_ref.shape
    tj = r_ref.shape[2]
    e = g_hbm.shape[2]
    pairs = chans // 2
    copies = [
        pltpu.make_async_copy(r_hbm, r_ref, sems.at[0]),
        pltpu.make_async_copy(l_hbm, l_ref, sems.at[1]),
        pltpu.make_async_copy(w_hbm, w_ref, sems.at[2]),
        pltpu.make_async_copy(g_hbm, gbd_ref.at[:, 0, :, pl.ds(0, e)], sems.at[3]),
        pltpu.make_async_copy(g_hbm, gbd_ref.at[:, 1, :, pl.ds(e, e)], sems.at[4]),
    ]
    for copy in copies:
        copy.start()
    zero = jnp.zeros((gbd_ref.shape[0], tj, e), BF16)
    gbd_ref[:, 0, :, e:] = zero
    gbd_ref[:, 1, :, :e] = zero
    copies[0].wait()
    per = 128 // tj
    for m in range(chans // per):
        r_out[:, m * 128 : (m + 1) * 128] = jnp.concatenate(
            [r_ref[m * per + k].astype(F32) for k in range(per)], axis=1
        ).astype(BF16)
    copies[1].wait()
    per = 128 // ti
    for m in range(chans // per):
        l_out[0, :, m * 128 : (m + 1) * 128] = jnp.concatenate(
            [l_ref[m * per + k].astype(F32) for k in range(per)], axis=1
        ).astype(BF16)
    copies[2].wait()
    swapped = jnp.swapaxes(w_ref[...].astype(F32).reshape(chans, chans, e), 0, 1).astype(BF16)
    for p in range(pairs):
        for d2 in range(2):
            wp[p * chans : (p + 1) * chans, d2 * e : (d2 + 1) * e] = swapped[2 * p + d2]
    copies[3].wait()
    copies[4].wait()


def outer_grad_kernel(gbd_ref, wp, y_ref):
    ti, _, tj, two_e = gbd_ref.shape
    lanes = 2 * tj
    pairs = y_ref.shape[1] // lanes
    chans = 2 * pairs
    for q in range(ti // 2):
        res = lax.dot_general(
            wp[...],
            gbd_ref[2 * q : 2 * q + 2].reshape(2 * lanes, two_e),
            (((1,), (1,)), ((), ())),
            preferred_element_type=F32,
        ).astype(BF16)
        for i in range(2):
            row = (2 * q + i) * chans
            for p in range(pairs):
                y_ref[row : row + chans, p * lanes : (p + 1) * lanes] = res[
                    p * chans : (p + 1) * chans, i * lanes : (i + 1) * lanes
                ]


def left_kernel(n_row, n_col, *refs):
    chips = n_row // 2
    r_refs = refs[:chips]
    y_ref, r_all, l_keep, l_mid, l_send, rblk, l_part = refs[chips:]
    row = lax.axis_index("row")
    col = lax.axis_index("col")
    core = row % 2
    chip = row // 2
    _, s_l, tall = l_keep.shape
    half = n_col // 2
    scale = 1.0 / (s_l * n_col)
    for k in range(chips):
        rblk[2 * k] = r_refs[k][0]
        rblk[2 * k + 1] = r_refs[k][1]
    r_all[...] = jnp.concatenate(
        [rblk[2 * ((p // 2) ^ chip) + ((p % 2) ^ core)] for p in range(n_row)], axis=0
    )
    span = tall // 4
    for n in range(4):
        res = lax.dot_general(
            r_all[...],
            y_ref[n * span : (n + 1) * span, :],
            (((1,), (1,)), ((), ())),
            preferred_element_type=F32,
        )
        for p in range(n_col):
            l_part[p ^ col, :, n * span : (n + 1) * span] = res[p * s_l : (p + 1) * s_l, :]
    for a in range(half // 2):
        l_keep[a] = l_part[4 * a]
        l_mid[a] = l_part[4 * a + 2]
        l_send[a] = (l_part[4 * a + 1] * scale).astype(BF16)
        l_send[half // 2 + a] = (l_part[4 * a + 3] * scale).astype(BF16)


def main_kernel(n_row, n_col, chans, *refs):
    l_near, l_far, r_all, gbd_ref, y_ref, keep_ref, send_ref = refs[:7]
    lblk, l_all, lt, x_ref, both = refs[7:]
    row = lax.axis_index("row")
    col = lax.axis_index("col")
    core = row % 2
    chip = row // 2
    _, _, tall = l_near.shape
    total, wide = r_all.shape
    s_r = total // n_row
    scale = 1.0 / total
    pairs = chans // 2
    lanes = wide // pairs
    ti = tall // chans
    per = ti // STEPS
    rows = per * chans
    two_e = gbd_ref.shape[3]
    own_c = chans // n_row

    for a, slot in enumerate(near_slots(n_col)):
        lblk[slot] = l_near[a]
        lblk[slot ^ 1] = l_far[a]
    by_chan = jnp.concatenate([lblk[p ^ col] for p in range(n_col)], axis=0).astype(F32).T
    lt[...] = (
        jnp.swapaxes(by_chan.reshape(chans, ti, total), 0, 1).reshape(tall, total).astype(BF16)
    )
    l_all[...] = lt[...].T
    tile = 2 * lanes

    def outer_step(n, carry):
        right = r_all[:, n * tile : (n + 1) * tile]
        for s in range(STEPS):
            res = jnp.dot(
                lt[s * rows : (s + 1) * rows, :], right, preferred_element_type=F32
            ).astype(BF16)
            for p in range(2):
                at = pl.ds((2 * n + p) * chans, chans)
                for i in range(per):
                    x_ref[at, (s * per + i) * lanes : (s * per + i + 1) * lanes] = res[
                        i * chans : (i + 1) * chans, p * lanes : (p + 1) * lanes
                    ]
        return carry

    for n in range(wide // tile):
        outer_step(n, 0)

    def place(r):
        return (r % 2) ^ core, (r // 2) ^ chip

    w_rows = pairs * own_c * two_e // wide
    height = pairs
    for first in range(0, pairs, height):
        res = jnp.dot(
            x_ref[first * chans : (first + height) * chans, :],
            gbd_ref[...].reshape(tall * wide // (pairs * chans), two_e),
            preferred_element_type=F32,
        ) * scale
        for r in range(n_row):
            piece = jnp.concatenate(
                [
                    res[p * chans + r * own_c : p * chans + (r + 1) * own_c, :]
                    for p in range(height)
                ],
                axis=0,
            )
            side, slot = place(r)
            for a in range(height * own_c // w_rows):
                at = first * own_c // w_rows + a
                both[side, slot, s_r : s_r + w_rows, at * two_e : (at + 1) * two_e] = piece[
                    a * w_rows : (a + 1) * w_rows, :
                ]

    span = wide // 4
    for n in range(4):
        res = (
            jnp.dot(
                l_all[...], y_ref[:, n * span : (n + 1) * span], preferred_element_type=F32
            )
            * scale
        )
        for r in range(n_row):
            side, slot = place(r)
            both[side, slot, :s_r, n * span : (n + 1) * span] = res[r * s_r : (r + 1) * s_r, :]
    keep_ref[...] = both[0]
    send_ref[...] = both[1]


def work(n_row, n_col, left_act, right_act, cotangent, weight):
    chans, s_l, ti = left_act.shape
    _, s_r, tj = right_act.shape
    e = cotangent.shape[2]
    chips = n_row // 2
    total = s_l * n_col
    pairs = chans // 2
    wide = chans * tj
    tall = chans * ti

    l_near, r_own, gbd, w_pairs = pl.pallas_call(
        prep_kernel,
        in_specs=[HBM] * 4,
        out_specs=[VMEM] * 4,
        out_shape=[
            jax.ShapeDtypeStruct((1, s_l, tall), BF16),
            jax.ShapeDtypeStruct((s_r, wide), BF16),
            jax.ShapeDtypeStruct((ti, 2, tj, 2 * e), BF16),
            jax.ShapeDtypeStruct((pairs * chans, 2 * e), BF16),
        ],
        scratch_shapes=[
            pltpu.VMEM((chans, s_l, ti), BF16),
            pltpu.VMEM((chans, s_r, tj), BF16),
            pltpu.VMEM((chans * chans, e), BF16),
            pltpu.SemaphoreType.DMA((5,)),
        ],
        compiler_params=pltpu.CompilerParams(vmem_limit_bytes=16 << 20),
    )(*[
        pltpu.with_memory_space_constraint(item, pltpu.HBM)
        for item in (left_act, right_act, cotangent, weight)
    ])
    r_other = xor_permute(r_own, "row", n_row, 1)
    half = n_col // 2
    far = half
    while far > 1:
        l_new = xor_permute(l_near, "col", n_col, far)
        l_near = jnp.concatenate([l_near, l_new])
        far //= 2
    r_pair = jnp.stack([r_own, r_other])
    r_set = [r_pair] + [xor_permute(r_pair, "row", n_row, 2 * k) for k in range(1, chips)]
    l_far = xor_permute(l_near, "col", n_col, 1)

    y = pl.pallas_call(
        outer_grad_kernel,
        in_specs=[VMEM] * 2,
        out_specs=VMEM,
        out_shape=jax.ShapeDtypeStruct((tall, wide), BF16),
        compiler_params=pltpu.CompilerParams(vmem_limit_bytes=16 << 20),
        cost_estimate=pl.CostEstimate(
            flops=4 * ti * tj * e * chans * chans, bytes_accessed=8 << 20, transcendentals=0
        ),
    )(gbd, w_pairs)

    w_rows = chans * chans * e // n_row // wide
    high = s_r + w_rows
    r_all, l_own, l_mid, l_send = pl.pallas_call(
        functools.partial(left_kernel, n_row, n_col),
        in_specs=[VMEM] * (chips + 1),
        out_specs=[VMEM] * 4,
        out_shape=[jax.ShapeDtypeStruct((total, wide), BF16)]
        + [jax.ShapeDtypeStruct((half // 2, s_l, tall), F32)] * 2
        + [jax.ShapeDtypeStruct((half, s_l, tall), BF16)],
        scratch_shapes=[
            pltpu.VMEM((n_row, s_r, wide), BF16),
            pltpu.VMEM((n_col, s_l, tall), F32),
        ],
        compiler_params=pltpu.CompilerParams(vmem_limit_bytes=16 << 20),
        cost_estimate=pl.CostEstimate(
            flops=2 * total * tall * wide, bytes_accessed=4 << 20, transcendentals=0
        ),
    )(*r_set, y)

    keep, send = pl.pallas_call(
        functools.partial(main_kernel, n_row, n_col, chans),
        in_specs=[VMEM] * 5,
        out_specs=[VMEM] * 2,
        out_shape=[jax.ShapeDtypeStruct((chips, high, wide), F32)] * 2,
        scratch_shapes=[
            pltpu.VMEM((n_col, s_l, tall), BF16),
            pltpu.VMEM((total, tall), BF16),
            pltpu.VMEM((tall, total), BF16),
            pltpu.VMEM((pairs * chans, 2 * ti * tj), BF16),
            pltpu.VMEM((2, chips, high, wide), F32),
        ],
        compiler_params=pltpu.CompilerParams(vmem_limit_bytes=24 << 20),
        cost_estimate=pl.CostEstimate(
            flops=6 * total * tall * wide, bytes_accessed=8 << 20, transcendentals=0
        ),
    )(l_near, l_far, r_all, gbd, y)

    other = xor_permute(send, "row", n_row, 1)
    l_got = xor_permute(l_send, "col", n_col, 1)
    l_mid = lax.optimization_barrier(l_mid * (1.0 / total))
    summed = keep + other
    row_sum = summed[0]
    got = [xor_permute(summed[k].astype(BF16), "row", n_row, 2 * k) for k in range(1, chips)]
    for item in got:
        row_sum = row_sum + item.astype(F32)

    part = half // 2
    l_new = xor_permute((l_mid + l_got[part:].astype(F32)).astype(BF16), "col", n_col, 2)
    l_own = lax.optimization_barrier(l_own * (1.0 / total))
    l_sum = l_own + l_got[:part].astype(F32) + l_new.astype(F32)
    far = 4
    while far < n_col:
        l_new = xor_permute(l_sum[1::2].astype(BF16), "col", n_col, far)
        l_sum = l_sum[0::2] + l_new.astype(F32)
        far *= 2

    r_sum, w_sum = lax.optimization_barrier((row_sum[:s_r], row_sum[s_r:]))
    far = 1
    while 2 * far < n_col:
        w_sum = w_sum + xor_permute(w_sum, "col", n_col, far)
        far *= 2
    w_own = w_sum.astype(BF16)
    w_sum = w_own.astype(F32) + xor_permute(w_own, "col", n_col, far).astype(F32)
    grad_right = r_sum.reshape(s_r, chans, tj).transpose(1, 0, 2)
    grad_left = l_sum.reshape(s_l, ti, chans).transpose(2, 0, 1)
    own_c = chans // n_row
    fold = wide // (2 * e)
    grad_weight = w_sum.reshape(w_rows, fold, 2, e).transpose(1, 0, 2, 3)
    grad_weight = (
        grad_weight.reshape(pairs, own_c, 2, e).transpose(1, 0, 2, 3).reshape(own_c * chans, e)
    )
    return grad_left, grad_right, grad_weight


def solution(mesh):
    return jax.shard_map(
        functools.partial(work, mesh.shape["row"], mesh.shape["col"]),
        mesh=mesh,
        in_specs=(P(None, "col", "row"), P(None, "row", "col"), P("row", "col", None), P()),
        out_specs=(P(None, "col", "row"), P(None, "row", "col"), P("row", None)),
        check_vma=False,
    )
```

profile of v0, /device:TPU:0, one launch (start us, length us, event | category | flops | bytes accessed | tf_op | source)
XLA Modules:
  0.0 38.0 jit_solution(10431083825592120081)
XLA Ops:
  0.6 1.4 %shard_map.67 = (bf16[1,16,1024]{2,1,0:T(8,128)(2,1)S(1)}, bf16[8,2048]{1,0:T(8,128)(2,1)S(1)}, bf16[32,2,64,256]{3,2,1,0:T(8,128)(2,1)S(1)}, bf16[512,256]{1,0:T(8,128)(2,1)S(1)}) custom-call(bf16[32,16,32]{2,1,0:T(8,128)(2,1)} %l_hbm.1, bf16[32,8,64]{2,1,0:T(8,128)(2,1)} %r_hbm.1, bf16[32,64,128]{2,1,0:T(8,128)(2,1)} %g_hbm.1, bf16[1024,128]{1,0:T(8,128)(2,1)} %w_hbm.1), custom_call_target="tpu_custom_call" | custom-call | tf_op jit(solution)/shard_map/pallas_call | solution.py:220
  2.1 0.6 %collective-permute-start = (bf16[8,2048]{1,0:T(8,128)(2,1)S(1)}, bf16[8,2048]{1,0:T(8,128)(2,1)S(1)}, u32[]{:S(2)}, u32[]{:S(2)}) collective-permute-start(bf16[8,2048]{1,0:T(8,128)(2,1)S(1)} %get-tuple-element.15), channel_id=1, source_target_pairs={{0,4},{4,0},{8,12},{12,8},{16,20},{20,16},{24,28},{28,24},{1,5},{5... | collective-permute-start | bytes 98312 | tf_op jit(solution)/shard_map/ppermute | solution.py:19
  2.6 3.7 %collective-permute-start.6 = (bf16[1,16,1024]{2,1,0:T(8,128)(2,1)S(1)}, bf16[1,16,1024]{2,1,0:T(8,128)(2,1)S(1)}, u32[]{:S(2)}, u32[]{:S(2)}) collective-permute-start(bf16[1,16,1024]{2,1,0:T(8,128)(2,1)S(1)} %get-tuple-element.21), channel_id=1, source_target_pairs={{0,2},{1,3},{2,0},{3,1},{4,6},{5,7},{6,4},{7,5},{8,10},{9,11},{10,... | collective-permute-start | bytes 98312 | tf_op jit(solution)/shard_map/ppermute | solution.py:19
  6.3 2.5 %collective-permute-start.3 = (bf16[2,8,2048]{2,1,0:T(8,128)(2,1)S(1)}, bf16[2,8,2048]{2,1,0:T(8,128)(2,1)S(1)}, u32[]{:S(2)}, u32[]{:S(2)}) collective-permute-start(bf16[2,8,2048]{2,1,0:T(8,128)(2,1)S(1)} %pad_maximum_fusion.refs_0_), channel_id=1, source_target_pairs={{0,24},{4,28},{8,16},{12,20},{16,8},{20,12},{24,0},{28,4},{1,25},{... | collective-permute-start | bytes 196616 | tf_op jit(solution)/shard_map/ppermute | solution.py:19
  8.8 0.5 %collective-permute-start.2 = (bf16[2,8,2048]{2,1,0:T(8,128)(2,1)S(1)}, bf16[2,8,2048]{2,1,0:T(8,128)(2,1)S(1)}, u32[]{:S(2)}, u32[]{:S(2)}) collective-permute-start(bf16[2,8,2048]{2,1,0:T(8,128)(2,1)S(1)} %pad_maximum_fusion.refs_0_), channel_id=1, source_target_pairs={{0,16},{4,20},{8,24},{12,28},{16,0},{20,4},{24,8},{28,12},{1,17},{... | collective-permute-start | bytes 196616 | tf_op jit(solution)/shard_map/ppermute | solution.py:19
  9.3 0.5 %collective-permute-start.1 = (bf16[2,8,2048]{2,1,0:T(8,128)(2,1)S(1)}, bf16[2,8,2048]{2,1,0:T(8,128)(2,1)S(1)}, u32[]{:S(2)}, u32[]{:S(2)}) collective-permute-start(bf16[2,8,2048]{2,1,0:T(8,128)(2,1)S(1)} %pad_maximum_fusion.refs_0_), channel_id=1, source_target_pairs={{0,8},{4,12},{8,0},{12,4},{16,24},{20,28},{24,16},{28,20},{1,9},{5... | collective-permute-start | bytes 196616 | tf_op jit(solution)/shard_map/ppermute | solution.py:19
  9.9 1.6 %collective-permute-start.7 = (bf16[2,16,1024]{2,1,0:T(8,128)(2,1)S(1)}, bf16[2,16,1024]{2,1,0:T(8,128)(2,1)S(1)}, u32[]{:S(2)}, u32[]{:S(2)}) collective-permute-start(bf16[2,16,1024]{2,1,0:T(8,128)(2,1)S(1)} %constant_dynamic-update-slice_fusion.refs_0_), channel_id=1, source_target_pairs={{0,1},{1,0},{2,3},{3,2},{4,5},{5,4},{6,7},{7,6},{8,9},{9,8},{10,11... | collective-permute-start | bytes 196616 | tf_op jit(solution)/shard_map/ppermute | solution.py:19
  11.4 1.6 %shard_map.68.refs_4_ = bf16[1024,2048]{1,0:T(8,128)(2,1)S(1)} custom-call(bf16[32,2,64,256]{3,2,1,0:T(8,128)(2,1)S(1)} %get-tuple-element.16.gbd_ref.refs_3_, bf16[512,256]{1,0:T(8,128)(2,1)S(1)} %get-tuple-element.17.wp), custom_call_target="tpu_custom_call" | custom-call | flops 1073741824 | bytes 8388608 | tf_op jit(solution)/shard_map/pallas_call | solution.py:252
  13.6 1.4 %shard_map.69 = (bf16[64,2048]{1,0:T(8,128)(2,1)S(1)}, f32[1,16,1024]{2,1,0:T(8,128)S(1)}, f32[1,16,1024]{2,1,0:T(8,128)S(1)}, bf16[2,16,1024]{2,1,0:T(8,128)(2,1)S(1)}) custom-call(bf16[2,8,2048]{2,1,0:T(8,128)(2,1)S(1)} %pad_maximum_fusion.refs_0_, bf16[2,8,2048]{2,1,0:T(8,128)(2,1)S(1)} %collective-permute-done.1.refs_1_, ...), custom_call_target="tpu_custom_call" | custom-call | flops 268435456 | bytes 4194304 | tf_op jit(solution)/shard_map/pallas_call | solution.py:265
  15.0 3.4 %shard_map.70 = (f32[4,16,2048]{2,1,0:T(8,128)S(1)}, f32[4,16,2048]{2,1,0:T(8,128)S(1)}) custom-call(bf16[2,16,1024]{2,1,0:T(8,128)(2,1)S(1)} %constant_dynamic-update-slice_fusion.refs_0_, bf16[2,16,1024]{2,1,0:T(8,128)(2,1)S(1)} %collective-permute-done.7.refs_1_, bf16[64,2048]{1,0:T(8,128)(2,1)S(1)} %get-tuple-element.22.refs_2_, ...), custom_call_target="tpu_custom_call" | custom-call | flops 805306368 | bytes 8388608 | tf_op jit(solution)/shard_map/pallas_call | solution.py:282
  18.5 1.9 %collective-permute-done.8 = f32[4,16,2048]{2,1,0:T(8,128)S(1)} collective-permute-done((f32[4,16,2048]{2,1,0:T(8,128)S(1)}, f32[4,16,2048]{2,1,0:T(8,128)S(1)}, u32[]{:S(2)}, u32[]{:S(2)}) %collective-permute-start.8) | collective-permute-done | bytes 524320 | tf_op jit(solution)/shard_map/ppermute | solution.py:19
  20.4 1.0 %collective-permute-start.9 = (bf16[16,2048]{1,0:T(8,128)(2,1)S(1)}, bf16[16,2048]{1,0:T(8,128)(2,1)S(1)}, u32[]{:S(2)}, u32[]{:S(2)}) collective-permute-start(bf16[16,2048]{1,0:T(8,128)(2,1)S(1)} %get-tuple-element.29), channel_id=1, source_target_pairs={{0,8},{4,12},{8,0},{12,4},{16,24},{20,28},{24,16},{28,20},{1,9},{5... | collective-permute-start | bytes 196616 | tf_op jit(solution)/shard_map/ppermute | solution.py:19
  21.4 2.0 %collective-permute-start.11 = (bf16[16,2048]{1,0:T(8,128)(2,1)S(1)}, bf16[16,2048]{1,0:T(8,128)(2,1)S(1)}, u32[]{:S(2)}, u32[]{:S(2)}) collective-permute-start(bf16[16,2048]{1,0:T(8,128)(2,1)S(1)} %get-tuple-element.30), channel_id=1, source_target_pairs={{0,24},{4,28},{8,16},{12,20},{16,8},{20,12},{24,0},{28,4},{1,25},{... | collective-permute-start | bytes 196616 | tf_op jit(solution)/shard_map/ppermute | solution.py:19
  24.0 1.6 %collective-permute-start.4 = (bf16[2,16,1024]{2,1,0:T(8,128)(2,1)S(1)}, bf16[2,16,1024]{2,1,0:T(8,128)(2,1)S(1)}, u32[]{:S(2)}, u32[]{:S(2)}) collective-permute-start(bf16[2,16,1024]{2,1,0:T(8,128)(2,1)S(1)} %get-tuple-element.19), channel_id=1, source_target_pairs={{0,1},{1,0},{2,3},{3,2},{4,5},{5,4},{6,7},{7,6},{8,9},{9,8},{10,11... | collective-permute-start | bytes 196616 | tf_op jit(solution)/shard_map/ppermute | solution.py:19
  25.6 1.5 %collective-permute-done.11 = bf16[16,2048]{1,0:T(8,128)(2,1)S(1)} collective-permute-done((bf16[16,2048]{1,0:T(8,128)(2,1)S(1)}, bf16[16,2048]{1,0:T(8,128)(2,1)S(1)}, u32[]{:S(2)}, u32[]{:S(2)}) %collective-permute-start.11) | collective-permute-done | bytes 65568 | tf_op jit(solution)/shard_map/ppermute | solution.py:19
  27.1 0.9 %collective-permute-done.10 = bf16[16,2048]{1,0:T(8,128)(2,1)S(1)} collective-permute-done((bf16[16,2048]{1,0:T(8,128)(2,1)S(1)}, bf16[16,2048]{1,0:T(8,128)(2,1)S(1)}, u32[]{:S(2)}, u32[]{:S(2)}) %collective-permute-start.10) | collective-permute-done | bytes 65568 | tf_op jit(solution)/shard_map/ppermute | solution.py:19
  28.1 1.6 %collective-permute-start.12 = (f32[8,2048]{1,0:T(8,128)S(1)}, f32[8,2048]{1,0:T(8,128)S(1)}, u32[]{:S(2)}, u32[]{:S(2)}) collective-permute-start(f32[8,2048]{1,0:T(8,128)S(1)} %get-tuple-element.26), channel_id=1, source_target_pairs={{0,1},{1,0},{2,3},{3,2},{4,5},{5,4},{6,7},{7,6},{8,9},{9,8},{10,11... | collective-permute-start | bytes 196616 | tf_op jit(solution)/shard_map/ppermute | solution.py:19
  29.7 1.3 %collective-permute-start.5 = (bf16[1,16,1024]{2,1,0:T(8,128)(2,1)S(1)}, bf16[1,16,1024]{2,1,0:T(8,128)(2,1)S(1)}, u32[]{:S(2)}, u32[]{:S(2)}) collective-permute-start(bf16[1,16,1024]{2,1,0:T(8,128)(2,1)S(1)} %add_convert_fusion.1), channel_id=1, source_target_pairs={{0,2},{1,3},{2,0},{3,1},{4,6},{5,7},{6,4},{7,5},{8,10},{9,11},{10,... | collective-permute-start | bytes 98312 | tf_op jit(solution)/shard_map/ppermute | solution.py:19
  31.0 1.4 %collective-permute-done.12 = f32[8,2048]{1,0:T(8,128)S(1)} collective-permute-done((f32[8,2048]{1,0:T(8,128)S(1)}, f32[8,2048]{1,0:T(8,128)S(1)}, u32[]{:S(2)}, u32[]{:S(2)}) %collective-permute-start.12) | collective-permute-done | bytes 65568 | tf_op jit(solution)/shard_map/ppermute | solution.py:19
  32.4 1.8 %collective-permute-start.13 = (bf16[8,2048]{1,0:T(8,128)(2,1)S(1)}, bf16[8,2048]{1,0:T(8,128)(2,1)S(1)}, u32[]{:S(2)}, u32[]{:S(2)}) collective-permute-start(bf16[8,2048]{1,0:T(8,128)(2,1)S(1)} %add_convert_fusion), channel_id=1, source_target_pairs={{0,2},{1,3},{2,0},{3,1},{4,6},{5,7},{6,4},{7,5},{8,10},{9,11},{10,... | collective-permute-start | bytes 98312 | tf_op jit(solution)/shard_map/ppermute | solution.py:19
  34.2 1.0 %collective-permute-done.5 = bf16[1,16,1024]{2,1,0:T(8,128)(2,1)S(1)} collective-permute-done((bf16[1,16,1024]{2,1,0:T(8,128)(2,1)S(1)}, bf16[1,16,1024]{2,1,0:T(8,128)(2,1)S(1)}, u32[]{:S(2)}, u32[]{:S(2)}) %collective-permute-start.5) | collective-permute-done | bytes 32800 | tf_op jit(solution)/shard_map/ppermute | solution.py:19
  35.3 0.9 %copy.12 = f32[16,32,32]{1,0,2:T(8,128)} copy(f32[16,32,32]{2,1,0:T(8,128)S(1)} %reshape.24) | data formatting | bytes 131072 | tf_op jit(solution)/shard_map/reshape | solution.py:327
  36.3 0.7 %copy.17 = f32[8,32,64]{2,0,1:T(8,128)} copy(f32[8,32,64]{2,1,0:T(8,128)S(1)} %reshape.25) | data formatting | bytes 131072 | tf_op jit(solution)/shard_map/reshape | solution.py:326
  37.3 0.7 %copy.15 = f32[4,16,2,128]{3,2,1,0:T(2,128)} copy(f32[4,16,2,128]{3,0,1,2:T(4,128)S(1)} %bitcast.30) | data formatting | bytes 131072 | tf_op jit(solution)/shard_map/transpose | solution.py:332
  (27 shorter events, 1.9 us)
Async XLA Ops:
  2.1 4.2 %collective-permute-start = (bf16[8,2048]{1,0:T(8,128)(2,1)S(1)}, bf16[8,2048]{1,0:T(8,128)(2,1)S(1)}, u32[]{:S(2)}, u32[]{:S(2)}) collective-permute-start(bf16[8,2048]{1,0:T(8,128)(2,1)S(1)} %get-tuple-element.15), channel_id=1, source_target_pairs={{0,4},{4,0},{8,12},{12,8},{16,20},{20,16},{24,28},{28,24},{1,5},{5... | collective-permute-start | bytes 98312 | tf_op jit(solution)/shard_map/ppermute | solution.py:19
  2.6 7.2 %collective-permute-start.6 = (bf16[1,16,1024]{2,1,0:T(8,128)(2,1)S(1)}, bf16[1,16,1024]{2,1,0:T(8,128)(2,1)S(1)}, u32[]{:S(2)}, u32[]{:S(2)}) collective-permute-start(bf16[1,16,1024]{2,1,0:T(8,128)(2,1)S(1)} %get-tuple-element.21), channel_id=1, source_target_pairs={{0,2},{1,3},{2,0},{3,1},{4,6},{5,7},{6,4},{7,5},{8,10},{9,11},{10,... | collective-permute-start | bytes 98312 | tf_op jit(solution)/shard_map/ppermute | solution.py:19
  6.3 6.7 %collective-permute-start.3 = (bf16[2,8,2048]{2,1,0:T(8,128)(2,1)S(1)}, bf16[2,8,2048]{2,1,0:T(8,128)(2,1)S(1)}, u32[]{:S(2)}, u32[]{:S(2)}) collective-permute-start(bf16[2,8,2048]{2,1,0:T(8,128)(2,1)S(1)} %pad_maximum_fusion.refs_0_), channel_id=1, source_target_pairs={{0,24},{4,28},{8,16},{12,20},{16,8},{20,12},{24,0},{28,4},{1,25},{... | collective-permute-start | bytes 196616 | tf_op jit(solution)/shard_map/ppermute | solution.py:19
  8.8 4.3 %collective-permute-start.2 = (bf16[2,8,2048]{2,1,0:T(8,128)(2,1)S(1)}, bf16[2,8,2048]{2,1,0:T(8,128)(2,1)S(1)}, u32[]{:S(2)}, u32[]{:S(2)}) collective-permute-start(bf16[2,8,2048]{2,1,0:T(8,128)(2,1)S(1)} %pad_maximum_fusion.refs_0_), channel_id=1, source_target_pairs={{0,16},{4,20},{8,24},{12,28},{16,0},{20,4},{24,8},{28,12},{1,17},{... | collective-permute-start | bytes 196616 | tf_op jit(solution)/shard_map/ppermute | solution.py:19
  9.3 4.3 %collective-permute-start.1 = (bf16[2,8,2048]{2,1,0:T(8,128)(2,1)S(1)}, bf16[2,8,2048]{2,1,0:T(8,128)(2,1)S(1)}, u32[]{:S(2)}, u32[]{:S(2)}) collective-permute-start(bf16[2,8,2048]{2,1,0:T(8,128)(2,1)S(1)} %pad_maximum_fusion.refs_0_), channel_id=1, source_target_pairs={{0,8},{4,12},{8,0},{12,4},{16,24},{20,28},{24,16},{28,20},{1,9},{5... | collective-permute-start | bytes 196616 | tf_op jit(solution)/shard_map/ppermute | solution.py:19
  9.9 5.1 %collective-permute-start.7 = (bf16[2,16,1024]{2,1,0:T(8,128)(2,1)S(1)}, bf16[2,16,1024]{2,1,0:T(8,128)(2,1)S(1)}, u32[]{:S(2)}, u32[]{:S(2)}) collective-permute-start(bf16[2,16,1024]{2,1,0:T(8,128)(2,1)S(1)} %constant_dynamic-update-slice_fusion.refs_0_), channel_id=1, source_target_pairs={{0,1},{1,0},{2,3},{3,2},{4,5},{5,4},{6,7},{7,6},{8,9},{9,8},{10,11... | collective-permute-start | bytes 196616 | tf_op jit(solution)/shard_map/ppermute | solution.py:19
  18.4 2.0 %collective-permute-start.8 = (f32[4,16,2048]{2,1,0:T(8,128)S(1)}, f32[4,16,2048]{2,1,0:T(8,128)S(1)}, u32[]{:S(2)}, u32[]{:S(2)}) collective-permute-start(f32[4,16,2048]{2,1,0:T(8,128)S(1)} %get-tuple-element.24), channel_id=1, source_target_pairs={{0,4},{4,0},{8,12},{12,8},{16,20},{20,16},{24,28},{28,24},{1,5},{5... | collective-permute-start | bytes 1572872 | tf_op jit(solution)/shard_map/ppermute | solution.py:19
  20.4 5.1 %collective-permute-start.9 = (bf16[16,2048]{1,0:T(8,128)(2,1)S(1)}, bf16[16,2048]{1,0:T(8,128)(2,1)S(1)}, u32[]{:S(2)}, u32[]{:S(2)}) collective-permute-start(bf16[16,2048]{1,0:T(8,128)(2,1)S(1)} %get-tuple-element.29), channel_id=1, source_target_pairs={{0,8},{4,12},{8,0},{12,4},{16,24},{20,28},{24,16},{28,20},{1,9},{5... | collective-permute-start | bytes 196616 | tf_op jit(solution)/shard_map/ppermute | solution.py:19
  21.4 5.7 %collective-permute-start.11 = (bf16[16,2048]{1,0:T(8,128)(2,1)S(1)}, bf16[16,2048]{1,0:T(8,128)(2,1)S(1)}, u32[]{:S(2)}, u32[]{:S(2)}) collective-permute-start(bf16[16,2048]{1,0:T(8,128)(2,1)S(1)} %get-tuple-element.30), channel_id=1, source_target_pairs={{0,24},{4,28},{8,16},{12,20},{16,8},{20,12},{24,0},{28,4},{1,25},{... | collective-permute-start | bytes 196616 | tf_op jit(solution)/shard_map/ppermute | solution.py:19
  23.5 4.5 %collective-permute-start.10 = (bf16[16,2048]{1,0:T(8,128)(2,1)S(1)}, bf16[16,2048]{1,0:T(8,128)(2,1)S(1)}, u32[]{:S(2)}, u32[]{:S(2)}) collective-permute-start(bf16[16,2048]{1,0:T(8,128)(2,1)S(1)} %get-tuple-element.31), channel_id=1, source_target_pairs={{0,16},{4,20},{8,24},{12,28},{16,0},{20,4},{24,8},{28,12},{1,17},{... | collective-permute-start | bytes 196616 | tf_op jit(solution)/shard_map/ppermute | solution.py:19
  24.0 5.7 %collective-permute-start.4 = (bf16[2,16,1024]{2,1,0:T(8,128)(2,1)S(1)}, bf16[2,16,1024]{2,1,0:T(8,128)(2,1)S(1)}, u32[]{:S(2)}, u32[]{:S(2)}) collective-permute-start(bf16[2,16,1024]{2,1,0:T(8,128)(2,1)S(1)} %get-tuple-element.19), channel_id=1, source_target_pairs={{0,1},{1,0},{2,3},{3,2},{4,5},{5,4},{6,7},{7,6},{8,9},{9,8},{10,11... | collective-permute-start | bytes 196616 | tf_op jit(solution)/shard_map/ppermute | solution.py:19
  28.1 4.3 %collective-permute-start.12 = (f32[8,2048]{1,0:T(8,128)S(1)}, f32[8,2048]{1,0:T(8,128)S(1)}, u32[]{:S(2)}, u32[]{:S(2)}) collective-permute-start(f32[8,2048]{1,0:T(8,128)S(1)} %get-tuple-element.26), channel_id=1, source_target_pairs={{0,1},{1,0},{2,3},{3,2},{4,5},{5,4},{6,7},{7,6},{8,9},{9,8},{10,11... | collective-permute-start | bytes 196616 | tf_op jit(solution)/shard_map/ppermute | solution.py:19
  29.7 5.5 %collective-permute-start.5 = (bf16[1,16,1024]{2,1,0:T(8,128)(2,1)S(1)}, bf16[1,16,1024]{2,1,0:T(8,128)(2,1)S(1)}, u32[]{:S(2)}, u32[]{:S(2)}) collective-permute-start(bf16[1,16,1024]{2,1,0:T(8,128)(2,1)S(1)} %add_convert_fusion.1), channel_id=1, source_target_pairs={{0,2},{1,3},{2,0},{3,1},{4,6},{5,7},{6,4},{7,5},{8,10},{9,11},{10,... | collective-permute-start | bytes 98312 | tf_op jit(solution)/shard_map/ppermute | solution.py:19
  32.4 4.9 %collective-permute-start.13 = (bf16[8,2048]{1,0:T(8,128)(2,1)S(1)}, bf16[8,2048]{1,0:T(8,128)(2,1)S(1)}, u32[]{:S(2)}, u32[]{:S(2)}) collective-permute-start(bf16[8,2048]{1,0:T(8,128)(2,1)S(1)} %add_convert_fusion), channel_id=1, source_target_pairs={{0,2},{1,3},{2,0},{3,1},{4,6},{5,7},{6,4},{7,5},{8,10},{9,11},{10,... | collective-permute-start | bytes 98312 | tf_op jit(solution)/shard_map/ppermute | solution.py:19
where the time goes:
time: 38.2 us; the launch traced here: 38 us
  starting transfers between devices  19.3 us (51%)
  Pallas kernels  7.75 us (20%)
  waiting for transfers between devices  7.58 us (20%)
  local copies, waits for them, and re-layouts  2.51 us (7%)
  between operations  0.76 us (2%)
    ppermute x14, starting transfers between devices, xor_permute(): return lax.ppermute(x, axis, [(r, r ^ k) for r in range(size)])  19.3 us
    ppermute x14, waiting for transfers between devices, xor_permute(): return lax.ppermute(x, axis, [(r, r ^ k) for r in range(size)])  7.58 us
    pallas_call x1, Pallas kernels, work(): pl.pallas_call(functools.partial(main_kernel, n_row, n_col, chans), in_sp...  3.35 us
    pallas_call x1, Pallas kernels, work(): pl.pallas_call(outer_grad_kernel, in_specs=[VMEM] * 2, out_specs=VMEM, ou...  1.56 us
    pallas_call x1, Pallas kernels, work(): pl.pallas_call(prep_kernel, in_specs=[HBM] * 4, out_specs=[VMEM] * 4, out...  1.43 us
    pallas_call x1, Pallas kernels, work(): pl.pallas_call(functools.partial(left_kernel, n_row, n_col), in_specs=[VM...  1.41 us
    reshape x2, local copies, waits for them, and re-layouts, work(): grad_left = l_sum.reshape(s_l, ti, chans).transpose(2, 0, 1)  0.97 us
    reshape x2, local copies, waits for them, and re-layouts, work(): grad_right = r_sum.reshape(s_r, chans, tj).transpose(1, 0, 2)  0.82 us
  transfers between devices with their start and end apart: 14, of which 8 were waited for; matrix products, arithmetic and copies ran while one was open for 5% of the time, Pallas kernels for 8%

commit v1 on v0

--- a/solution.py
+++ b/solution.py
@@ -28,23 +28,17 @@
     return slots
 
 
-def prep_kernel(l_hbm, r_hbm, g_hbm, w_hbm, l_out, r_out, gbd_ref, wp, l_ref, r_ref, w_ref, sems):
+def prep_kernel(l_hbm, r_hbm, g_hbm, w_hbm, l_out, r_out, g_ref, w_ref, l_ref, r_ref, sems):
     chans, _, ti = l_ref.shape
     tj = r_ref.shape[2]
-    e = g_hbm.shape[2]
-    pairs = chans // 2
     copies = [
         pltpu.make_async_copy(r_hbm, r_ref, sems.at[0]),
         pltpu.make_async_copy(l_hbm, l_ref, sems.at[1]),
         pltpu.make_async_copy(w_hbm, w_ref, sems.at[2]),
-        pltpu.make_async_copy(g_hbm, gbd_ref.at[:, 0, :, pl.ds(0, e)], sems.at[3]),
-        pltpu.make_async_copy(g_hbm, gbd_ref.at[:, 1, :, pl.ds(e, e)], sems.at[4]),
+        pltpu.make_async_copy(g_hbm, g_ref, sems.at[3]),
     ]
     for copy in copies:
         copy.start()
-    zero = jnp.zeros((gbd_ref.shape[0], tj, e), BF16)
-    gbd_ref[:, 0, :, e:] = zero
-    gbd_ref[:, 1, :, :e] = zero
     copies[0].wait()
     per = 128 // tj
     for m in range(chans // per):
@@ -58,23 +52,29 @@
             [l_ref[m * per + k].astype(F32) for k in range(per)], axis=1
         ).astype(BF16)
     copies[2].wait()
+    copies[3].wait()
+
+
+def outer_grad_kernel(g_ref, w_ref, y_ref, gbd_ref, wp):
+    ti, tj, e = g_ref.shape
+    lanes = 2 * tj
+    pairs = y_ref.shape[1] // lanes
+    chans = 2 * pairs
+    zero = jnp.zeros((tj, e), BF16)
     swapped = jnp.swapaxes(w_ref[...].astype(F32).reshape(chans, chans, e), 0, 1).astype(BF16)
     for p in range(pairs):
         for d2 in range(2):
             wp[p * chans : (p + 1) * chans, d2 * e : (d2 + 1) * e] = swapped[2 * p + d2]
-    copies[3].wait()
-    copies[4].wait()
-
-
-def outer_grad_kernel(gbd_ref, wp, y_ref):
-    ti, _, tj, two_e = gbd_ref.shape
-    lanes = 2 * tj
-    pairs = y_ref.shape[1] // lanes
-    chans = 2 * pairs
     for q in range(ti // 2):
+        for i in (2 * q, 2 * q + 1):
+            block = g_ref[i]
+            gbd_ref[i, 0, :, :e] = block
+            gbd_ref[i, 0, :, e:] = zero
+            gbd_ref[i, 1, :, :e] = zero
+            gbd_ref[i, 1, :, e:] = block
         res = lax.dot_general(
             wp[...],
-            gbd_ref[2 * q : 2 * q + 2].reshape(2 * lanes, two_e),
+            gbd_ref[2 * q : 2 * q + 2].reshape(2 * lanes, 2 * e),
             (((1,), (1,)), ((), ())),
             preferred_element_type=F32,
         ).astype(BF16)
@@ -106,11 +106,11 @@
     span = tall // 4
     for n in range(4):
         res = lax.dot_general(
+            y_ref[n * span : (n + 1) * span, :],
             r_all[...],
-            y_ref[n * span : (n + 1) * span, :],
             (((1,), (1,)), ((), ())),
             preferred_element_type=F32,
-        )
+        ).T
         for p in range(n_col):
             l_part[p ^ col, :, n * span : (n + 1) * span] = res[p * s_l : (p + 1) * s_l, :]
     for a in range(half // 2):
@@ -217,21 +217,20 @@
     wide = chans * tj
     tall = chans * ti
 
-    l_near, r_own, gbd, w_pairs = pl.pallas_call(
+    l_near, r_own, g_near, w_near = pl.pallas_call(
         prep_kernel,
         in_specs=[HBM] * 4,
         out_specs=[VMEM] * 4,
         out_shape=[
             jax.ShapeDtypeStruct((1, s_l, tall), BF16),
             jax.ShapeDtypeStruct((s_r, wide), BF16),
-            jax.ShapeDtypeStruct((ti, 2, tj, 2 * e), BF16),
-            jax.ShapeDtypeStruct((pairs * chans, 2 * e), BF16),
+            jax.ShapeDtypeStruct((ti, tj, e), BF16),
+            jax.ShapeDtypeStruct((chans * chans, e), BF16),
         ],
         scratch_shapes=[
             pltpu.VMEM((chans, s_l, ti), BF16),
             pltpu.VMEM((chans, s_r, tj), BF16),
-            pltpu.VMEM((chans * chans, e), BF16),
-            pltpu.SemaphoreType.DMA((5,)),
+            pltpu.SemaphoreType.DMA((4,)),
         ],
         compiler_params=pltpu.CompilerParams(vmem_limit_bytes=16 << 20),
     )(*[
@@ -246,19 +245,25 @@
         l_near = jnp.concatenate([l_near, l_new])
         far //= 2
     r_pair = jnp.stack([r_own, r_other])
-    r_set = [r_pair] + [xor_permute(r_pair, "row", n_row, 2 * k) for k in range(1, chips)]
+    r_set = [r_pair]
+    for k in range(1, chips):
+        r_set.append(xor_permute(r_pair, "row", n_row, 2 * k))
     l_far = xor_permute(l_near, "col", n_col, 1)
 
-    y = pl.pallas_call(
+    y, gbd = pl.pallas_call(
         outer_grad_kernel,
         in_specs=[VMEM] * 2,
-        out_specs=VMEM,
-        out_shape=jax.ShapeDtypeStruct((tall, wide), BF16),
+        out_specs=[VMEM] * 2,
+        out_shape=[
+            jax.ShapeDtypeStruct((tall, wide), BF16),
+            jax.ShapeDtypeStruct((ti, 2, tj, 2 * e), BF16),
+        ],
+        scratch_shapes=[pltpu.VMEM((pairs * chans, 2 * e), BF16)],
         compiler_params=pltpu.CompilerParams(vmem_limit_bytes=16 << 20),
         cost_estimate=pl.CostEstimate(
             flops=4 * ti * tj * e * chans * chans, bytes_accessed=8 << 20, transcendentals=0
         ),
-    )(gbd, w_pairs)
+    )(g_near, w_near)
 
     w_rows = chans * chans * e // n_row // wide
     high = s_r + w_rows
@@ -302,7 +307,9 @@
     l_mid = lax.optimization_barrier(l_mid * (1.0 / total))
     summed = keep + other
     row_sum = summed[0]
-    got = [xor_permute(summed[k].astype(BF16), "row", n_row, 2 * k) for k in range(1, chips)]
+    got = []
+    for k in range(1, chips):
+        got.append(xor_permute(summed[k].astype(BF16), "row", n_row, 2 * k))
     for item in got:
         row_sum = row_sum + item.astype(F32)
 

time: 38.2 us -> 37.9 us (level)
  transfers between devices with their start and end apart: 14 -> 14, of which waited for: 8 -> 7; matrix products, arithmetic and copies ran while one was open for 5% -> 5% of each run, Pallas kernels for 8% -> 8%
where the time goes in v1:
time: 37.9 us; the launch traced here: 37.8 us
  starting transfers between devices  19.3 us (51%)
  Pallas kernels  7.62 us (20%)
  waiting for transfers between devices  7.44 us (20%)
  local copies, waits for them, and re-layouts  2.51 us (7%)
  between operations  0.77 us (2%)
    ppermute x14, starting transfers between devices, xor_permute(): return lax.ppermute(x, axis, [(r, r ^ k) for r in range(size)])  19.3 us
    ppermute x14, waiting for transfers between devices, xor_permute(): return lax.ppermute(x, axis, [(r, r ^ k) for r in range(size)])  7.44 us
    pallas_call x1, Pallas kernels, work(): pl.pallas_call(functools.partial(main_kernel, n_row, n_col, chans), in_sp...  3.35 us
    pallas_call x1, Pallas kernels, work(): pl.pallas_call(outer_grad_kernel, in_specs=[VMEM] * 2, out_specs=[VMEM] *...  1.65 us
    pallas_call x1, Pallas kernels, work(): pl.pallas_call(functools.partial(left_kernel, n_row, n_col), in_specs=[VM...  1.35 us
    pallas_call x1, Pallas kernels, work(): pl.pallas_call(prep_kernel, in_specs=[HBM] * 4, out_specs=[VMEM] * 4, out...  1.26 us
    reshape x2, local copies, waits for them, and re-layouts, work(): grad_left = l_sum.reshape(s_l, ti, chans).transpose(2, 0, 1)  0.97 us
    reshape x2, local copies, waits for them, and re-layouts, work(): grad_right = r_sum.reshape(s_r, chans, tj).transpose(1, 0, 2)  0.82 us
  transfers between devices with their start and end apart: 14, of which 7 were waited for; matrix products, arithmetic and copies ran while one was open for 5% of the time, Pallas kernels for 8%

profile of v1, /device:TPU:0, one launch (start us, length us, event | category | flops | bytes accessed | tf_op | source)
XLA Modules:
  0.0 37.8 jit_solution(6545652335139270257)
XLA Ops:
  0.6 1.3 %shard_map.67 = (bf16[1,16,1024]{2,1,0:T(8,128)(2,1)S(1)}, bf16[8,2048]{1,0:T(8,128)(2,1)S(1)}, bf16[32,64,128]{2,1,0:T(8,128)(2,1)S(1)}, bf16[1024,128]{1,0:T(8,128)(2,1)S(1)}) custom-call(bf16[32,16,32]{2,1,0:T(8,128)(2,1)} %l_hbm.1, bf16[32,8,64]{2,1,0:T(8,128)(2,1)} %r_hbm.1, bf16[32,64,128]{2,1,0:T(8,128)(2,1)} %g_hbm.1, bf16[1024,128]{1,0:T(8,128)(2,1)} %w_hbm.1), custom_call_target="tpu_custom_call" | custom-call | tf_op jit(solution)/shard_map/pallas_call | solution.py:220
  1.9 0.6 %collective-permute-start = (bf16[8,2048]{1,0:T(8,128)(2,1)S(1)}, bf16[8,2048]{1,0:T(8,128)(2,1)S(1)}, u32[]{:S(2)}, u32[]{:S(2)}) collective-permute-start(bf16[8,2048]{1,0:T(8,128)(2,1)S(1)} %get-tuple-element.17), channel_id=1, source_target_pairs={{0,4},{4,0},{8,12},{12,8},{16,20},{20,16},{24,28},{28,24},{1,5},{5... | collective-permute-start | bytes 98312 | tf_op jit(solution)/shard_map/ppermute | solution.py:19
  2.5 3.7 %collective-permute-start.6 = (bf16[1,16,1024]{2,1,0:T(8,128)(2,1)S(1)}, bf16[1,16,1024]{2,1,0:T(8,128)(2,1)S(1)}, u32[]{:S(2)}, u32[]{:S(2)}) collective-permute-start(bf16[1,16,1024]{2,1,0:T(8,128)(2,1)S(1)} %get-tuple-element.24), channel_id=1, source_target_pairs={{0,2},{1,3},{2,0},{3,1},{4,6},{5,7},{6,4},{7,5},{8,10},{9,11},{10,... | collective-permute-start | bytes 98312 | tf_op jit(solution)/shard_map/ppermute | solution.py:19
  6.1 2.5 %collective-permute-start.3 = (bf16[2,8,2048]{2,1,0:T(8,128)(2,1)S(1)}, bf16[2,8,2048]{2,1,0:T(8,128)(2,1)S(1)}, u32[]{:S(2)}, u32[]{:S(2)}) collective-permute-start(bf16[2,8,2048]{2,1,0:T(8,128)(2,1)S(1)} %pad_maximum_fusion.refs_0_), channel_id=1, source_target_pairs={{0,24},{4,28},{8,16},{12,20},{16,8},{20,12},{24,0},{28,4},{1,25},{... | collective-permute-start | bytes 196616 | tf_op jit(solution)/shard_map/ppermute | solution.py:19
  8.6 0.5 %collective-permute-start.2 = (bf16[2,8,2048]{2,1,0:T(8,128)(2,1)S(1)}, bf16[2,8,2048]{2,1,0:T(8,128)(2,1)S(1)}, u32[]{:S(2)}, u32[]{:S(2)}) collective-permute-start(bf16[2,8,2048]{2,1,0:T(8,128)(2,1)S(1)} %pad_maximum_fusion.refs_0_), channel_id=1, source_target_pairs={{0,16},{4,20},{8,24},{12,28},{16,0},{20,4},{24,8},{28,12},{1,17},{... | collective-permute-start | bytes 196616 | tf_op jit(solution)/shard_map/ppermute | solution.py:19
  9.1 0.5 %collective-permute-start.1 = (bf16[2,8,2048]{2,1,0:T(8,128)(2,1)S(1)}, bf16[2,8,2048]{2,1,0:T(8,128)(2,1)S(1)}, u32[]{:S(2)}, u32[]{:S(2)}) collective-permute-start(bf16[2,8,2048]{2,1,0:T(8,128)(2,1)S(1)} %pad_maximum_fusion.refs_0_), channel_id=1, source_target_pairs={{0,8},{4,12},{8,0},{12,4},{16,24},{20,28},{24,16},{28,20},{1,9},{5... | collective-permute-start | bytes 196616 | tf_op jit(solution)/shard_map/ppermute | solution.py:19
  9.7 1.6 %collective-permute-start.7 = (bf16[2,16,1024]{2,1,0:T(8,128)(2,1)S(1)}, bf16[2,16,1024]{2,1,0:T(8,128)(2,1)S(1)}, u32[]{:S(2)}, u32[]{:S(2)}) collective-permute-start(bf16[2,16,1024]{2,1,0:T(8,128)(2,1)S(1)} %constant_dynamic-update-slice_fusion.refs_0_), channel_id=1, source_target_pairs={{0,1},{1,0},{2,3},{3,2},{4,5},{5,4},{6,7},{7,6},{8,9},{9,8},{10,11... | collective-permute-start | bytes 196616 | tf_op jit(solution)/shard_map/ppermute | solution.py:19
  11.3 1.7 %shard_map.68 = (bf16[1024,2048]{1,0:T(8,128)(2,1)S(1)}, bf16[32,2,64,256]{3,2,1,0:T(8,128)(2,1)S(1)}) custom-call(bf16[32,64,128]{2,1,0:T(8,128)(2,1)S(1)} %get-tuple-element.18.g_ref, bf16[1024,128]{1,0:T(8,128)(2,1)S(1)} %get-tuple-element.19.w_ref), custom_call_target="tpu_custom_call" | custom-call | flops 1073741824 | bytes 8388608 | tf_op jit(solution)/shard_map/pallas_call | solution.py:253
  13.4 1.4 %shard_map.69 = (bf16[64,2048]{1,0:T(8,128)(2,1)S(1)}, f32[1,16,1024]{2,1,0:T(8,128)S(1)}, f32[1,16,1024]{2,1,0:T(8,128)S(1)}, bf16[2,16,1024]{2,1,0:T(8,128)(2,1)S(1)}) custom-call(bf16[2,8,2048]{2,1,0:T(8,128)(2,1)S(1)} %pad_maximum_fusion.refs_0_, bf16[2,8,2048]{2,1,0:T(8,128)(2,1)S(1)} %collective-permute-done.1.refs_1_, ...), custom_call_target="tpu_custom_call" | custom-call | flops 268435456 | bytes 4194304 | tf_op jit(solution)/shard_map/pallas_call | solution.py:270
  14.8 3.4 %shard_map.70 = (f32[4,16,2048]{2,1,0:T(8,128)S(1)}, f32[4,16,2048]{2,1,0:T(8,128)S(1)}) custom-call(bf16[2,16,1024]{2,1,0:T(8,128)(2,1)S(1)} %constant_dynamic-update-slice_fusion.refs_0_, bf16[2,16,1024]{2,1,0:T(8,128)(2,1)S(1)} %collective-permute-done.7.refs_1_, bf16[64,2048]{1,0:T(8,128)(2,1)S(1)} %get-tuple-element.25.refs_2_, ...), custom_call_target="tpu_custom_call" | custom-call | flops 805306368 | bytes 8388608 | tf_op jit(solution)/shard_map/pallas_call | solution.py:287
  18.2 1.9 %collective-permute-done.8 = f32[4,16,2048]{2,1,0:T(8,128)S(1)} collective-permute-done((f32[4,16,2048]{2,1,0:T(8,128)S(1)}, f32[4,16,2048]{2,1,0:T(8,128)S(1)}, u32[]{:S(2)}, u32[]{:S(2)}) %collective-permute-start.8) | collective-permute-done | bytes 524320 | tf_op jit(solution)/shard_map/ppermute | solution.py:19
  20.2 1.1 %collective-permute-start.9 = (bf16[16,2048]{1,0:T(8,128)(2,1)S(1)}, bf16[16,2048]{1,0:T(8,128)(2,1)S(1)}, u32[]{:S(2)}, u32[]{:S(2)}) collective-permute-start(bf16[16,2048]{1,0:T(8,128)(2,1)S(1)} %get-tuple-element.33), channel_id=1, source_target_pairs={{0,8},{4,12},{8,0},{12,4},{16,24},{20,28},{24,16},{28,20},{1,9},{5... | collective-permute-start | bytes 196616 | tf_op jit(solution)/shard_map/ppermute | solution.py:19
  21.3 1.9 %collective-permute-start.11 = (bf16[16,2048]{1,0:T(8,128)(2,1)S(1)}, bf16[16,2048]{1,0:T(8,128)(2,1)S(1)}, u32[]{:S(2)}, u32[]{:S(2)}) collective-permute-start(bf16[16,2048]{1,0:T(8,128)(2,1)S(1)} %get-tuple-element.34), channel_id=1, source_target_pairs={{0,24},{4,28},{8,16},{12,20},{16,8},{20,12},{24,0},{28,4},{1,25},{... | collective-permute-start | bytes 196616 | tf_op jit(solution)/shard_map/ppermute | solution.py:19
  23.8 1.6 %collective-permute-start.4 = (bf16[2,16,1024]{2,1,0:T(8,128)(2,1)S(1)}, bf16[2,16,1024]{2,1,0:T(8,128)(2,1)S(1)}, u32[]{:S(2)}, u32[]{:S(2)}) collective-permute-start(bf16[2,16,1024]{2,1,0:T(8,128)(2,1)S(1)} %get-tuple-element.22), channel_id=1, source_target_pairs={{0,1},{1,0},{2,3},{3,2},{4,5},{5,4},{6,7},{7,6},{8,9},{9,8},{10,11... | collective-permute-start | bytes 196616 | tf_op jit(solution)/shard_map/ppermute | solution.py:19
  25.4 1.5 %collective-permute-done.11 = bf16[16,2048]{1,0:T(8,128)(2,1)S(1)} collective-permute-done((bf16[16,2048]{1,0:T(8,128)(2,1)S(1)}, bf16[16,2048]{1,0:T(8,128)(2,1)S(1)}, u32[]{:S(2)}, u32[]{:S(2)}) %collective-permute-start.11) | collective-permute-done | bytes 65568 | tf_op jit(solution)/shard_map/ppermute | solution.py:19
  26.9 0.9 %collective-permute-done.10 = bf16[16,2048]{1,0:T(8,128)(2,1)S(1)} collective-permute-done((bf16[16,2048]{1,0:T(8,128)(2,1)S(1)}, bf16[16,2048]{1,0:T(8,128)(2,1)S(1)}, u32[]{:S(2)}, u32[]{:S(2)}) %collective-permute-start.10) | collective-permute-done | bytes 65568 | tf_op jit(solution)/shard_map/ppermute | solution.py:19
  27.8 1.6 %collective-permute-start.12 = (f32[8,2048]{1,0:T(8,128)S(1)}, f32[8,2048]{1,0:T(8,128)S(1)}, u32[]{:S(2)}, u32[]{:S(2)}) collective-permute-start(f32[8,2048]{1,0:T(8,128)S(1)} %get-tuple-element.30), channel_id=1, source_target_pairs={{0,1},{1,0},{2,3},{3,2},{4,5},{5,4},{6,7},{7,6},{8,9},{9,8},{10,11... | collective-permute-start | bytes 196616 | tf_op jit(solution)/shard_map/ppermute | solution.py:19
  29.5 1.3 %collective-permute-start.5 = (bf16[1,16,1024]{2,1,0:T(8,128)(2,1)S(1)}, bf16[1,16,1024]{2,1,0:T(8,128)(2,1)S(1)}, u32[]{:S(2)}, u32[]{:S(2)}) collective-permute-start(bf16[1,16,1024]{2,1,0:T(8,128)(2,1)S(1)} %add_convert_fusion.1), channel_id=1, source_target_pairs={{0,2},{1,3},{2,0},{3,1},{4,6},{5,7},{6,4},{7,5},{8,10},{9,11},{10,... | collective-permute-start | bytes 98312 | tf_op jit(solution)/shard_map/ppermute | solution.py:19
  30.8 1.4 %collective-permute-done.12 = f32[8,2048]{1,0:T(8,128)S(1)} collective-permute-done((f32[8,2048]{1,0:T(8,128)S(1)}, f32[8,2048]{1,0:T(8,128)S(1)}, u32[]{:S(2)}, u32[]{:S(2)}) %collective-permute-start.12) | collective-permute-done | bytes 65568 | tf_op jit(solution)/shard_map/ppermute | solution.py:19
  32.2 1.8 %collective-permute-start.13 = (bf16[8,2048]{1,0:T(8,128)(2,1)S(1)}, bf16[8,2048]{1,0:T(8,128)(2,1)S(1)}, u32[]{:S(2)}, u32[]{:S(2)}) collective-permute-start(bf16[8,2048]{1,0:T(8,128)(2,1)S(1)} %add_convert_fusion), channel_id=1, source_target_pairs={{0,2},{1,3},{2,0},{3,1},{4,6},{5,7},{6,4},{7,5},{8,10},{9,11},{10,... | collective-permute-start | bytes 98312 | tf_op jit(solution)/shard_map/ppermute | solution.py:19
  34.0 1.0 %collective-permute-done.5 = bf16[1,16,1024]{2,1,0:T(8,128)(2,1)S(1)} collective-permute-done((bf16[1,16,1024]{2,1,0:T(8,128)(2,1)S(1)}, bf16[1,16,1024]{2,1,0:T(8,128)(2,1)S(1)}, u32[]{:S(2)}, u32[]{:S(2)}) %collective-permute-start.5) | collective-permute-done | bytes 32800 | tf_op jit(solution)/shard_map/ppermute | solution.py:19
  35.1 0.9 %copy.12 = f32[16,32,32]{1,0,2:T(8,128)} copy(f32[16,32,32]{2,1,0:T(8,128)S(1)} %reshape.24) | data formatting | bytes 131072 | tf_op jit(solution)/shard_map/reshape | solution.py:334
  36.0 0.7 %copy.17 = f32[8,32,64]{2,0,1:T(8,128)} copy(f32[8,32,64]{2,1,0:T(8,128)S(1)} %reshape.25) | data formatting | bytes 131072 | tf_op jit(solution)/shard_map/reshape | solution.py:333
  37.1 0.7 %copy.15 = f32[4,16,2,128]{3,2,1,0:T(2,128)} copy(f32[4,16,2,128]{3,0,1,2:T(4,128)S(1)} %bitcast.30) | data formatting | bytes 131072 | tf_op jit(solution)/shard_map/transpose | solution.py:339
  (27 shorter events, 1.8 us)
Async XLA Ops:
  1.9 4.2 %collective-permute-start = (bf16[8,2048]{1,0:T(8,128)(2,1)S(1)}, bf16[8,2048]{1,0:T(8,128)(2,1)S(1)}, u32[]{:S(2)}, u32[]{:S(2)}) collective-permute-start(bf16[8,2048]{1,0:T(8,128)(2,1)S(1)} %get-tuple-element.17), channel_id=1, source_target_pairs={{0,4},{4,0},{8,12},{12,8},{16,20},{20,16},{24,28},{28,24},{1,5},{5... | collective-permute-start | bytes 98312 | tf_op jit(solution)/shard_map/ppermute | solution.py:19
  2.5 7.2 %collective-permute-start.6 = (bf16[1,16,1024]{2,1,0:T(8,128)(2,1)S(1)}, bf16[1,16,1024]{2,1,0:T(8,128)(2,1)S(1)}, u32[]{:S(2)}, u32[]{:S(2)}) collective-permute-start(bf16[1,16,1024]{2,1,0:T(8,128)(2,1)S(1)} %get-tuple-element.24), channel_id=1, source_target_pairs={{0,2},{1,3},{2,0},{3,1},{4,6},{5,7},{6,4},{7,5},{8,10},{9,11},{10,... | collective-permute-start | bytes 98312 | tf_op jit(solution)/shard_map/ppermute | solution.py:19
  6.1 6.8 %collective-permute-start.3 = (bf16[2,8,2048]{2,1,0:T(8,128)(2,1)S(1)}, bf16[2,8,2048]{2,1,0:T(8,128)(2,1)S(1)}, u32[]{:S(2)}, u32[]{:S(2)}) collective-permute-start(bf16[2,8,2048]{2,1,0:T(8,128)(2,1)S(1)} %pad_maximum_fusion.refs_0_), channel_id=1, source_target_pairs={{0,24},{4,28},{8,16},{12,20},{16,8},{20,12},{24,0},{28,4},{1,25},{... | collective-permute-start | bytes 196616 | tf_op jit(solution)/shard_map/ppermute | solution.py:19
  8.6 4.3 %collective-permute-start.2 = (bf16[2,8,2048]{2,1,0:T(8,128)(2,1)S(1)}, bf16[2,8,2048]{2,1,0:T(8,128)(2,1)S(1)}, u32[]{:S(2)}, u32[]{:S(2)}) collective-permute-start(bf16[2,8,2048]{2,1,0:T(8,128)(2,1)S(1)} %pad_maximum_fusion.refs_0_), channel_id=1, source_target_pairs={{0,16},{4,20},{8,24},{12,28},{16,0},{20,4},{24,8},{28,12},{1,17},{... | collective-permute-start | bytes 196616 | tf_op jit(solution)/shard_map/ppermute | solution.py:19
  9.1 4.3 %collective-permute-start.1 = (bf16[2,8,2048]{2,1,0:T(8,128)(2,1)S(1)}, bf16[2,8,2048]{2,1,0:T(8,128)(2,1)S(1)}, u32[]{:S(2)}, u32[]{:S(2)}) collective-permute-start(bf16[2,8,2048]{2,1,0:T(8,128)(2,1)S(1)} %pad_maximum_fusion.refs_0_), channel_id=1, source_target_pairs={{0,8},{4,12},{8,0},{12,4},{16,24},{20,28},{24,16},{28,20},{1,9},{5... | collective-permute-start | bytes 196616 | tf_op jit(solution)/shard_map/ppermute | solution.py:19
  9.7 5.1 %collective-permute-start.7 = (bf16[2,16,1024]{2,1,0:T(8,128)(2,1)S(1)}, bf16[2,16,1024]{2,1,0:T(8,128)(2,1)S(1)}, u32[]{:S(2)}, u32[]{:S(2)}) collective-permute-start(bf16[2,16,1024]{2,1,0:T(8,128)(2,1)S(1)} %constant_dynamic-update-slice_fusion.refs_0_), channel_id=1, source_target_pairs={{0,1},{1,0},{2,3},{3,2},{4,5},{5,4},{6,7},{7,6},{8,9},{9,8},{10,11... | collective-permute-start | bytes 196616 | tf_op jit(solution)/shard_map/ppermute | solution.py:19
  18.1 2.0 %collective-permute-start.8 = (f32[4,16,2048]{2,1,0:T(8,128)S(1)}, f32[4,16,2048]{2,1,0:T(8,128)S(1)}, u32[]{:S(2)}, u32[]{:S(2)}) collective-permute-start(f32[4,16,2048]{2,1,0:T(8,128)S(1)} %get-tuple-element.28), channel_id=1, source_target_pairs={{0,4},{4,0},{8,12},{12,8},{16,20},{20,16},{24,28},{28,24},{1,5},{5... | collective-permute-start | bytes 1572872 | tf_op jit(solution)/shard_map/ppermute | solution.py:19
  20.2 5.1 %collective-permute-start.9 = (bf16[16,2048]{1,0:T(8,128)(2,1)S(1)}, bf16[16,2048]{1,0:T(8,128)(2,1)S(1)}, u32[]{:S(2)}, u32[]{:S(2)}) collective-permute-start(bf16[16,2048]{1,0:T(8,128)(2,1)S(1)} %get-tuple-element.33), channel_id=1, source_target_pairs={{0,8},{4,12},{8,0},{12,4},{16,24},{20,28},{24,16},{28,20},{1,9},{5... | collective-permute-start | bytes 196616 | tf_op jit(solution)/shard_map/ppermute | solution.py:19
  21.3 5.6 %collective-permute-start.11 = (bf16[16,2048]{1,0:T(8,128)(2,1)S(1)}, bf16[16,2048]{1,0:T(8,128)(2,1)S(1)}, u32[]{:S(2)}, u32[]{:S(2)}) collective-permute-start(bf16[16,2048]{1,0:T(8,128)(2,1)S(1)} %get-tuple-element.34), channel_id=1, source_target_pairs={{0,24},{4,28},{8,16},{12,20},{16,8},{20,12},{24,0},{28,4},{1,25},{... | collective-permute-start | bytes 196616 | tf_op jit(solution)/shard_map/ppermute | solution.py:19
  23.3 4.5 %collective-permute-start.10 = (bf16[16,2048]{1,0:T(8,128)(2,1)S(1)}, bf16[16,2048]{1,0:T(8,128)(2,1)S(1)}, u32[]{:S(2)}, u32[]{:S(2)}) collective-permute-start(bf16[16,2048]{1,0:T(8,128)(2,1)S(1)} %get-tuple-element.35), channel_id=1, source_target_pairs={{0,16},{4,20},{8,24},{12,28},{16,0},{20,4},{24,8},{28,12},{1,17},{... | collective-permute-start | bytes 196616 | tf_op jit(solution)/shard_map/ppermute | solution.py:19
  23.8 5.7 %collective-permute-start.4 = (bf16[2,16,1024]{2,1,0:T(8,128)(2,1)S(1)}, bf16[2,16,1024]{2,1,0:T(8,128)(2,1)S(1)}, u32[]{:S(2)}, u32[]{:S(2)}) collective-permute-start(bf16[2,16,1024]{2,1,0:T(8,128)(2,1)S(1)} %get-tuple-element.22), channel_id=1, source_target_pairs={{0,1},{1,0},{2,3},{3,2},{4,5},{5,4},{6,7},{7,6},{8,9},{9,8},{10,11... | collective-permute-start | bytes 196616 | tf_op jit(solution)/shard_map/ppermute | solution.py:19
  27.8 4.3 %collective-permute-start.12 = (f32[8,2048]{1,0:T(8,128)S(1)}, f32[8,2048]{1,0:T(8,128)S(1)}, u32[]{:S(2)}, u32[]{:S(2)}) collective-permute-start(f32[8,2048]{1,0:T(8,128)S(1)} %get-tuple-element.30), channel_id=1, source_target_pairs={{0,1},{1,0},{2,3},{3,2},{4,5},{5,4},{6,7},{7,6},{8,9},{9,8},{10,11... | collective-permute-start | bytes 196616 | tf_op jit(solution)/shard_map/ppermute | solution.py:19
  29.5 5.5 %collective-permute-start.5 = (bf16[1,16,1024]{2,1,0:T(8,128)(2,1)S(1)}, bf16[1,16,1024]{2,1,0:T(8,128)(2,1)S(1)}, u32[]{:S(2)}, u32[]{:S(2)}) collective-permute-start(bf16[1,16,1024]{2,1,0:T(8,128)(2,1)S(1)} %add_convert_fusion.1), channel_id=1, source_target_pairs={{0,2},{1,3},{2,0},{3,1},{4,6},{5,7},{6,4},{7,5},{8,10},{9,11},{10,... | collective-permute-start | bytes 98312 | tf_op jit(solution)/shard_map/ppermute | solution.py:19
  32.2 4.9 %collective-permute-start.13 = (bf16[8,2048]{1,0:T(8,128)(2,1)S(1)}, bf16[8,2048]{1,0:T(8,128)(2,1)S(1)}, u32[]{:S(2)}, u32[]{:S(2)}) collective-permute-start(bf16[8,2048]{1,0:T(8,128)(2,1)S(1)} %add_convert_fusion), channel_id=1, source_target_pairs={{0,2},{1,3},{2,0},{3,1},{4,6},{5,7},{6,4},{7,5},{8,10},{9,11},{10,... | collective-permute-start | bytes 98312 | tf_op jit(solution)/shard_map/ppermute | solution.py:19
